TPU v7x, 32 devices: a whole 2x2x4 slice. The times are simulated.
32 devices in a mesh: dp: 8 (over y, x, core), tensor: 4 (over z).
Axes of the slice: x: 2, y: 2, z: 4, core: 2. Of those that a mesh axis runs over, the one named last changes fastest.
Arguments:
- tokens: bfloat16 [8192, 1024], P('dp'), may hold values from -6 to 6
- cotangent: bfloat16 [8192, 1024], P('dp'), may hold values from -6 to 6
- seq_lengths: int32 [8, 8], P('dp'), may hold values from 0 to 1024, as said below
- norm_gain: float32 [1024], replicated, may hold values from 0.5 to 1.5
- proj_gate: bfloat16 [1024, 2048], P(None, 'tensor'), may hold values from -0.1875 to 0.1875
- proj_value: bfloat16 [1024, 2048], P(None, 'tensor'), may hold values from -0.1875 to 0.1875
- proj_pair: bfloat16 [1024, 256], replicated, may hold values from -0.1875 to 0.1875
- proj_step: bfloat16 [1024, 32], P(None, 'tensor'), may hold values from -0.1875 to 0.1875
- conv_value: float32 [4, 2048], P(None, 'tensor'), may hold values from -3 to 3
- conv_value_bias: float32 [2048], P('tensor'), may hold values from -0.5 to 0.5
- conv_pair: float32 [4, 256], replicated, may hold values from -3 to 3
- conv_pair_bias: float32 [256], replicated, may hold values from -0.5 to 0.5
- step_bias: float32 [32], P('tensor'), may hold values from -4 to -1
- log_rate: float32 [32], P('tensor'), may hold values from 0 to 2.8
- skip_gain: float32 [32], P('tensor'), may hold values from 0.5 to 1.5
- gate_gain: float32 [2048], P('tensor'), may hold values from 0.5 to 1.5
- proj_out: bfloat16 [2048, 1024], P('tensor'), may hold values from -0.125 to 0.125
Outputs:
- block_out: bfloat16 [8192, 1024], P(('dp', 'tensor'))
- grad_tokens: bfloat16 [8192, 1024], P('dp')
- grad_norm_gain: float32 [1024], replicated
- grad_proj_gate: float32 [1024, 2048], P(None, 'tensor')
- grad_proj_value: float32 [1024, 2048], P(None, 'tensor')
- grad_proj_pair: float32 [1024, 256], replicated
- grad_proj_step: float32 [1024, 32], P(None, 'tensor')
- grad_conv_value: float32 [4, 2048], P(None, 'tensor')
- grad_conv_value_bias: float32 [2048], P('tensor')
- grad_conv_pair: float32 [4, 256], replicated
- grad_conv_pair_bias: float32 [256], replicated
- grad_step_bias: float32 [32], P('tensor')
- grad_log_rate: float32 [32], P('tensor')
- grad_skip_gain: float32 [32], P('tensor')
- grad_gate_gain: float32 [2048], P('tensor')
- grad_proj_out: float32 [2048, 1024], P('tensor')
Inputs may be any that keep to these rules, and one draw needn't show every extreme that they name: `seq_lengths`: row p lists the lengths of the sequences packed in order from the first of the 1024 rows of pack p; a zero is an unused slot; each row sums to at most 1024, and rows past that sum are padding.
All inputs are finite; a program needn't handle non-finite values.
Results may differ from a plain program's by a relative error of at most 0.0098.
Values sent between devices are 32-bit elements; how exact they have to be, the bound alone decides.
No kernel may reach another device: no remote copies, remote signals or barrier semaphores. Data moves between devices by JAX's collectives and lax.ppermute only.
A program may use at most 128 MiB of HBM per device.

v0:
```python
from functools import partial

import jax
import jax.numpy as jnp
from jax import lax
from jax.sharding import PartitionSpec as P

D = 1024
GROUP = 256
DI = 2048


epsilon = 1e-05
HIGHEST = lax.Precision.HIGHEST


def segment_ids(lengths_row, row_count):
    bounds = jnp.cumsum(lengths_row)
    position = jnp.arange(row_count, dtype=jnp.int32)
    segment = jnp.sum((position[:, None] >= bounds[None, :]).astype(jnp.int32), axis=1)
    live_mask = (position < bounds[-1]).astype(jnp.float32)
    return (segment, live_mask)


def conv_silu(pre_act, weight, conv_bias, segment):
    row_count = pre_act.shape[0]
    tap_count = weight.shape[0]
    summed = conv_bias[None, :] + weight[tap_count - 1][None, :] * pre_act
    for offset in range(1, tap_count):
        shifted = jnp.pad(pre_act, ((offset, 0), (0, 0)))[:row_count]
        shifted_seg = jnp.pad(segment, (offset, 0), constant_values=-1)[:row_count]
        same_seq = (shifted_seg == segment).astype(jnp.float32)
        summed = summed + weight[tap_count - 1 - offset][None, :] * shifted * same_seq[:, None]
    return jax.nn.silu(summed)


def ssd_gate(gate_pre, value_post, pair_post, step_pre, step_bias, log_rate, skip_gain, segment):
    row_count = value_post.shape[0]
    head_count = step_pre.shape[1]
    head_dim = value_post.shape[1] // head_count
    state_dim = pair_post.shape[1] // 2
    block_count = row_count // GROUP
    step_size = jax.nn.softplus(step_pre + step_bias[None, :])
    rate_per = -jnp.exp(log_rate)
    log_decay = step_size * rate_per[None, :]
    values = value_post.reshape(row_count, head_count, head_dim)
    scaled = (values * step_size[:, :, None]).reshape(block_count, GROUP, head_count, head_dim)
    cumulative = jnp.cumsum(log_decay.reshape(block_count, GROUP, head_count), axis=1)
    seg_blocks = segment.reshape(block_count, GROUP)
    b_blocks = pair_post[:, :state_dim].reshape(block_count, GROUP, state_dim)
    c_blocks = pair_post[:, state_dim:].reshape(block_count, GROUP, state_dim)
    lower_tri = jnp.arange(GROUP)[:, None] >= jnp.arange(GROUP)[None, :]
    same_seq = (seg_blocks[:, :, None] == seg_blocks[:, None, :]) & lower_tri[None]
    log_gap = cumulative[:, :, None, :] - cumulative[:, None, :, :]
    decay_mat = jnp.where(
        same_seq[..., None], jnp.exp(jnp.where(same_seq[..., None], log_gap, 0.0)), 0.0
    )
    scores = jnp.einsum("cin,cjn->cij", c_blocks, b_blocks, precision=HIGHEST)
    weights = scores[..., None] * decay_mat
    intra_out = jnp.einsum("cijh,cjhp->cihp", weights, scaled, precision=HIGHEST)
    before = jnp.concatenate([jnp.full((1,), -1, jnp.int32), seg_blocks[:-1, -1]])
    end_same = (seg_blocks == seg_blocks[:, -1:]).astype(jnp.float32)
    to_end = jnp.exp(cumulative[:, -1:, :] - cumulative) * end_same[:, :, None]
    local_states = jnp.einsum("cjh,cjn,cjhp->chnp", to_end, b_blocks, scaled, precision=HIGHEST)
    carry_in = jnp.exp(cumulative) * (seg_blocks == before[:, None]).astype(jnp.float32)[:, :, None]
    passes = (
        jnp.exp(cumulative[:, -1, :]) * (seg_blocks[:, -1] == before).astype(jnp.float32)[:, None]
    )

    def advance(state_now, inputs):
        c_block, carry_row, local_state, pass_row = inputs
        inter_out = (
            jnp.einsum("in,hnp->ihp", c_block, state_now, precision=HIGHEST) * carry_row[:, :, None]
        )
        return (local_state + pass_row[:, None, None] * state_now, inter_out)

    start_state = jnp.zeros((head_count, state_dim, head_dim), jnp.float32)
    final_state, inter_all = lax.scan(
        advance, start_state, (c_blocks, carry_in, local_states, passes)
    )
    mixed_out = (intra_out + inter_all).reshape(row_count, head_count * head_dim)
    mixed_out = mixed_out + jnp.repeat(skip_gain, head_dim)[None, :] * value_post
    return mixed_out * jax.nn.silu(gate_pre)


def mixer_rest(
    gate_pre,
    value_pre,
    pair_post,
    step_pre,
    conv_value,
    conv_value_bias,
    step_bias,
    log_rate,
    skip_gain,
    segment,
):
    value_post = conv_silu(value_pre, conv_value, conv_value_bias, segment)
    return ssd_gate(
        gate_pre, value_post, pair_post, step_pre, step_bias, log_rate, skip_gain, segment
    )


def per_device(
    tokens,
    cotangent,
    seq_lengths,
    norm_gain,
    proj_gate,
    proj_value,
    proj_pair,
    proj_step,
    conv_value,
    conv_value_bias,
    conv_pair,
    conv_pair_bias,
    step_bias,
    log_rate,
    skip_gain,
    gate_gain,
    proj_out,
):
    row_count = tokens.shape[0]
    segment, live_mask = segment_ids(seq_lengths[0], row_count)
    widened = tokens.astype(jnp.float32)
    scale_in = lax.rsqrt(jnp.mean(widened * widened, axis=1, keepdims=True) + epsilon)
    normed = (widened * scale_in * norm_gain[None, :]).astype(jnp.bfloat16)
    gate_pre = jnp.dot(normed, proj_gate, preferred_element_type=jnp.float32)
    value_pre = jnp.dot(normed, proj_value, preferred_element_type=jnp.float32)
    pair_pre = jnp.dot(normed, proj_pair, preferred_element_type=jnp.float32)
    step_pre = jnp.dot(normed, proj_step, preferred_element_type=jnp.float32)
    pair_post = conv_silu(pair_pre, conv_pair, conv_pair_bias, segment)
    rest_fn = partial(mixer_rest, segment=segment)
    gated_value, rest_back = jax.vjp(
        rest_fn,
        gate_pre,
        value_pre,
        pair_post,
        step_pre,
        conv_value,
        conv_value_bias,
        step_bias,
        log_rate,
        skip_gain,
    )
    square_sum = lax.psum(jnp.sum(gated_value * gated_value, axis=1), "tensor")
    scale_gate = lax.rsqrt(square_sum[:, None] / DI + epsilon)
    gate_out = (gated_value * scale_gate * gate_gain[None, :]).astype(jnp.bfloat16)
    share_rows = row_count // lax.axis_size("tensor")
    first_row = lax.axis_index("tensor") * share_rows
    mixed_rows = lax.psum_scatter(
        jnp.dot(gate_out, proj_out, preferred_element_type=jnp.float32),
        "tensor",
        scatter_dimension=0,
        tiled=True,
    )
    own_rows = lax.dynamic_slice_in_dim(widened, first_row, share_rows, 0)
    own_live = lax.dynamic_slice_in_dim(live_mask, first_row, share_rows, 0)
    block_out = (own_rows + mixed_rows * own_live[:, None]).astype(jnp.bfloat16)
    cot_live = jnp.where(live_mask[:, None] > 0, cotangent, jnp.zeros_like(cotangent))
    grad_proj_out = jnp.dot(gate_out.T, cot_live, preferred_element_type=jnp.float32)
    grad_gate_out = jnp.dot(cot_live, proj_out.T, preferred_element_type=jnp.float32)
    grad_gate_gain = jnp.sum(grad_gate_out * gated_value * scale_gate, axis=0)
    weighted = grad_gate_out * gate_gain[None, :]
    stat_dot = lax.psum(jnp.sum(weighted * gated_value, axis=1), "tensor")[:, None]
    grad_gated = weighted * scale_gate - gated_value * (scale_gate**3 / DI) * stat_dot
    grads_rest = rest_back(grad_gated)
    low_gate = grads_rest[0].astype(jnp.bfloat16)
    low_value = grads_rest[1].astype(jnp.bfloat16)
    low_step = grads_rest[3].astype(jnp.bfloat16)
    grad_proj_gate = jnp.dot(normed.T, low_gate, preferred_element_type=jnp.float32)
    grad_proj_value = jnp.dot(normed.T, low_value, preferred_element_type=jnp.float32)
    grad_proj_step = jnp.dot(normed.T, low_step, preferred_element_type=jnp.float32)
    grad_local = jnp.dot(low_gate, proj_gate.T, preferred_element_type=jnp.float32)
    grad_local = grad_local + jnp.dot(low_value, proj_value.T, preferred_element_type=jnp.float32)
    grad_local = grad_local + jnp.dot(low_step, proj_step.T, preferred_element_type=jnp.float32)
    pair_grad = lax.psum(grads_rest[2], "tensor")
    pair_fn = partial(conv_silu, segment=segment)
    whole_post, pair_back = jax.vjp(pair_fn, pair_pre, conv_pair, conv_pair_bias)
    grad_pair_pre, grad_conv_pair, grad_conv_pair_bias = pair_back(pair_grad)
    low_pair = grad_pair_pre.astype(jnp.bfloat16)
    grad_proj_pair = jnp.dot(normed.T, low_pair, preferred_element_type=jnp.float32)
    grad_normed = lax.psum(grad_local, "tensor")
    grad_normed = grad_normed + jnp.dot(low_pair, proj_pair.T, preferred_element_type=jnp.float32)
    grad_norm_gain = jnp.sum(grad_normed * widened * scale_in, axis=0)
    scaled_grad = grad_normed * norm_gain[None, :]
    row_dot = jnp.sum(scaled_grad * widened, axis=1, keepdims=True)
    grad_wide = scaled_grad * scale_in - widened * (scale_in**3 / D) * row_dot
    grad_tokens = (cotangent.astype(jnp.float32) + grad_wide).astype(jnp.bfloat16)
    totals = lax.psum(
        (
            grad_norm_gain,
            grad_proj_gate,
            grad_proj_value,
            grad_proj_step,
            grads_rest[4],
            grads_rest[5],
            grads_rest[6],
            grads_rest[7],
            grads_rest[8],
            grad_gate_gain,
            grad_proj_out,
            grad_proj_pair,
            grad_conv_pair,
            grad_conv_pair_bias,
        ),
        "dp",
    )
    pair_totals = (totals[11], totals[12], totals[13])
    return (
        block_out,
        grad_tokens,
        totals[0],
        totals[1],
        totals[2],
        pair_totals[0],
        totals[3],
        totals[4],
        totals[5],
        pair_totals[1],
        pair_totals[2],
        totals[6],
        totals[7],
        totals[8],
        totals[9],
        totals[10],
    )


def solution(mesh):
    return jax.shard_map(
        per_device,
        mesh=mesh,
        in_specs=(
            P("dp", None),
            P("dp", None),
            P("dp", None),
            P(),
            P(None, "tensor"),
            P(None, "tensor"),
            P(),
            P(None, "tensor"),
            P(None, "tensor"),
            P("tensor"),
            P(),
            P(),
            P("tensor"),
            P("tensor"),
            P("tensor"),
            P("tensor"),
            P("tensor", None),
        ),
        out_specs=(
            P(("dp", "tensor"), None),
            P("dp", None),
            P(),
            P(None, "tensor"),
            P(None, "tensor"),
            P(),
            P(None, "tensor"),
            P(None, "tensor"),
            P("tensor"),
            P(),
            P(),
            P("tensor"),
            P("tensor"),
            P("tensor"),
            P("tensor"),
            P("tensor", None),
        ),
        check_vma=False,
    )
```

profile of v0, /device:TPU:0, one launch (start us, length us, event | category | flops | bytes accessed | tf_op | source)
XLA Modules:
  0.0 684.8 jit_solution(3664673852586571083)
XLA Ops:
  17.0 2.3 reduce-window.19
  21.1 2.9 fusion.141
  24.0 2.8 fusion.61
  28.2 2.4 reshape.353
  30.5 2.8 copy.116
  33.4 3.2 fusion.142
  40.4 3.0 fusion.79
  44.6 27.7 %while.44 = (s32[]{:T(128)}, f32[8,128,64]{1,2,0:T(8,128)}, f32[4,256,8,64]{1,3,2,0:T(8,128)}, f32[4,8,128,64]{2,3,1,0:T(8,128)}, f32[4,256,8,1]{1,2,3,0:T(8,128...) while((s32[]{:T(128)}, f32[8,128,64]{1,2,0:T(8,128)}, ...), condition=%wide.region_6.7_spmd.clone, body=%wide.region_5.6_spmd.clone.sunk | while | flops 201654272 | bytes 4632367 | solution.py:78
  72.3 2.3 fusion.143
  75.8 10.8 %bitcast_add_fusion.2 = f32[4,256,8,64]{1,3,2,0:T(8,128)} fusion(f32[4,256,8,64]{1,3,2,0:T(8,128)S(1)} %copy-done.90, f32[4,256,8]{1,2,0:T(8,128)S(1)} %get-tuple-element.561, f32[4,256,256]{2,1,0:T(8,128)S(1)} %fusion.143, pred[4,256,256]{2,1,0:T(8,128)(4,1)S(1)} %compare_and_fusion, f32[4,256,8,64]{1,3,2,0:T(8,128)S(1)} %copy.116, ...), kind=kOutput, calls=%fused_computation.96 | convolution fusion | flops 1620049920 | bytes 7667712 | tf_op jit(solution)/shard_map/jvp(cijh,cjhp->cihp)/dot_general | solution.py:60
  86.6 3.8 copy.144
  90.5 5.3 reshape.354
  95.9 6.3 multiply_reduce_fusion.10
  102.2 13.5 %psum.126 = f32[1024]{0:T(1024)S(1)} all-reduce(f32[1024]{0:T(1024)S(1)} %get-tuple-element.558), channel_id=1, replica_groups=mesh['dp'=8,'tensor'=4] {'tensor'}, use_global_device_ids=true, to_apply=%region_8.9 | all-reduce | flops 1024 | bytes 8192 | tf_op jit(solution)/shard_map/psum | solution.py:146
  116.3 6.0 multiply_reduce_fusion.2
  122.4 8.3 %psum.127 = f32[1024]{0:T(1024)S(1)} all-reduce(f32[1024]{0:T(1024)S(1)} %get-tuple-element.477), channel_id=1, replica_groups=mesh['dp'=8,'tensor'=4] {'tensor'}, use_global_device_ids=true, to_apply=%region_11.12 | all-reduce | flops 1024 | bytes 8192 | tf_op jit(solution)/shard_map/psum | solution.py:165
  130.7 6.2 multiply_reduce_fusion.3
  136.9 2.9 copy.121
  139.8 3.3 reshape.324
  145.6 40.1 %while.45 = (s32[]{:T(128)}, f32[8,128,64]{1,2,0:T(8,128)S(1)}, f32[4,256,128]{2,1,0:T(8,128)}, f32[4,256,8]{1,2,0:T(8,128)S(1)}, f32[4,8,128,64]{2,3,1,0:T(8,12...) while((s32[]{:T(128)}, f32[8,128,64]{1,2,0:T(8,128)S(1)}, ...), condition=%wide.region_15.16_spmd.clone, body=%wide.region_12.15_spmd.clone.sunk | while | flops 403634176 | bytes 5301641 | solution.py:78
  145.6 2.1 constant_dynamic-slice_fusion.4
  186.3 6.5 fusion.82
  192.8 3.3 multiply_reduce_fusion.1
  196.1 3.0 copy.127
  199.0 14.8 %fusion.30 = (f32[4,256,8]{1,2,0:T(8,128)}, f32[4,256,8]{1,2,0:T(8,128)}, f32[4,256,256]{2,1,0:T(8,128)S(1)}) fusion(f32[4,256,8]{1,2,0:T(8,128)S(1)} %get-tuple-element.561, f32[4,256,256]{2,1,0:T(8,128)} %copy-done.36, pred[4,256,256]{2,1,0:T(8,128)(4,1)S(1)} %copy-done.40, f32[4,256,8,64]{1,3,2,0:T(8,128)S(1)} %copy-done.4, ...), kind=kOutput, calls=%fused_computation.55 | convolution fusion | flops 1633927168 | bytes 6684672 | tf_op jit(solution)/shard_map/transpose(jvp(cijh,cjhp->cihp))/dot_general | solution.py:60
  213.9 3.0 convolution_add_fusion.2
  216.9 2.7 convolution_add_fusion.1
  225.9 10.6 %reduce-window.21 = f32[4,8,2,128]{3,1,2,0:T(8,128)S(1)} reduce-window(f32[4,8,2,128]{3,1,2,0:T(8,128)} %add_bitcast_fusion, f32[]{:T(128)} %constant.146.clone.1), window={size=1x1x1x128 pad=0_0x0_0x0_0x0_127}, to_apply=%region_20.21 | reduce-window | flops 1040384 | bytes 65540 | tf_op jit(solution)/shard_map/reduce-window.3
  238.6 9.9 %bitcast_add_fusion.1 = f32[4,256,8,64]{1,3,2,0:T(8,128)} fusion(f32[4,256,8,64]{1,3,2,0:T(8,128)} %get-tuple-element.603, f32[4,256,8]{1,2,0:T(8,128)S(1)} %get-tuple-element.561, f32[4,256,256]{2,1,0:T(8,128)} %copy-done.36, pred[4,256,256]{2,1,0:T(8,128)(4,1)S(1)} %copy-done.40, f32[4,8,64,256]{3,0,2,1:T(4,128)S(1)} %bitcast.248, ...), kind=kOutput, calls=%fused_computation.95 | convolution fusion | flops 1620049920 | bytes 7667712 | tf_op jit(solution)/shard_map/transpose(jvp(cijh,cjhp->cihp))/dot_general | solution.py:60
  248.5 4.0 copy.145
  254.1 4.8 reshape.355
  260.5 3.1 copy.126
  263.6 7.2 %multiply_reduce_fusion.7 = (f32[512]{0:T(512)S(1)}, f32[512]{0:T(512)S(1)}, f32[512]{0:T(512)S(1)}, f32[512]{0:T(512)S(1)}, f32[512]{0:T(512)S(1)}, /*index=5*/f32[1024,512]{1,0:T(8,128)S(1)}) fusion(f32[1024,512]{1,0:T(8,128)} %copy-done.21, f32[1024]{0:T(1024)S(1)} %get-tuple-element.598, f32[1024]{0:T(1024)S(1)} %get-tuple-element.597, ...), kind=kLoop, calls=%fused_computation.103 | loop fusion | flops 12580352 | bytes 12607488 | tf_op jit(solution)/shard_map/transpose(jvp())/reduce_sum | solution.py:33
  278.9 2.7 add_add_fusion
  283.3 4.9 fusion.130
  289.7 3.9 fusion.147
  293.7 2.6 fusion.146
  296.3 2.8 fusion.102
  299.1 171.3 %all-reduce.35.cloned.1.call-done = (f32[1024,1024]{1,0:T(8,128)}, f32[1024,256]{1,0:T(8,128)}) async-done(((f32[1024,1024]{1,0:T(8,128)}, f32[1024,256]{1,0:T(8,128)}), (f32[1024,1024]{1,0:T(8,128)}, f32[1024,256]{1,0:T(8,128)})) %all-reduce.35.cloned.1.call-update) | async-done | bytes 5242896 | tf_op jit(solution)/shard_map/psum | solution.py:183
  470.4 3.9 multiply_reduce_fusion.14
  479.7 2.4 convert_element_type.89
  485.2 5.6 fusion.40
  490.8 26.2 %all-reduce.27 = (f32[1024]{0:T(1024)}, f32[1024,8]{0,1:T(8,128)}, f32[4,512]{1,0:T(4,128)}, f32[512]{0:T(512)}, f32[4,256]{1,0:T(4,128)}, /*index=5*/f32[256]{0...) all-reduce(f32[1024]{0:T(1024)S(1)} %get-tuple-element.474, ...), channel_id=1, replica_groups=mesh['dp'=8,'tensor'=4] {'dp'}, use_global_device_ids=true, to_apply=%region_27.28 | all-reduce | flops 13592 | bytes 108736 | tf_op jit(solution)/shard_map/psum | solution.py:190
  517.1 4.6 fusion.37
  521.7 26.8 %reduce-scatter.2.cloned.1.call-done = f32[256,1024]{1,0:T(8,128)} async-done(((f32[1024,1024]{1,0:T(8,128)}), f32[256,1024]{1,0:T(8,128)}) %reduce-scatter.2.cloned.1.call-update) | async-done | bytes 1048592 | tf_op jit(solution)/shard_map/reduce_scatter | solution.py:151
  548.5 2.5 add_convert_fusion
  551.0 118.4 %all-reduce.33.cloned.1.call-done = (f32[1024,512]{1,0:T(8,128)}, f32[1024,512]{1,0:T(8,128)}, f32[1024,256]{1,0:T(8,128)}, f32[512,1024]{1,0:T(8,128)}) async-done(((f32[1024,512]{1,0:T(8,128)}, f32[1024,512]{1,0:T(8,128)}, f32[1024,256]{1,0:T(8,128)}, f32[512,1024]{1,0:T(8,128)}), (f32[1024,512]{1,0:T(8,128)}, f32[1024,512]{1,0:T(8,128)}, f32[1024,256]{1,0:T(8,128)}, ...) | async-done | bytes 7340048 | tf_op jit(solution)/shard_map/psum | solution.py:190
  669.4 3.2 copy.229
  (355 shorter events, 124.7 us)
Async XLA Ops:
  7.2 88.7 %copy-start = (bf16[1024,512]{1,0:T(8,128)(2,1)S(1)}, bf16[1024,512]{1,0:T(8,128)(2,1)}, u32[]{:S(2)}) copy-start(bf16[1024,512]{1,0:T(8,128)(2,1)} %param.25) | copy-start | bytes 3145732
  7.2 6.7 copy-start.1
  7.2 6.1 copy-start.93
  7.2 6.7 copy-start.53
  7.2 463.2 %all-reduce.35.cloned.1.call-start = ((), (), s32[]{:S(2)}) async-start(), calls=%async_computation.3 | async-start | bytes 10485760 | tf_op jit(solution)/shard_map/psum | solution.py:183
  15.8 5.3 copy-start.91
  20.3 3.7 copy-start.55
  33.4 41.6 %copy-start.3 = (f32[4,256,8,64]{1,3,2,0:T(8,128)}, f32[4,256,8,64]{1,3,2,0:T(8,128)S(1)}, u32[]{:S(2)}) copy-start(f32[4,256,8,64]{1,3,2,0:T(8,128)S(1)} %copy.116) | copy-start | bytes 6291460
  33.4 3.2 copy-start.81
  33.4 3.2 copy-start.87
  39.5 5.1 copy-start.12
  44.6 3.3 copy-start.84
  50.8 4.3 copy-start.84
  58.0 4.3 copy-start.84
  65.2 4.3 copy-start.84
  72.3 3.5 copy-start.90
  90.5 5.3 copy-start.88
  90.5 5.4 copy-start.7
  95.9 34.8 %copy-start.66 = (f32[512]{0:T(512)}, f32[512]{0:T(512)S(1)}, u32[]{:S(2)}) copy-start(f32[512]{0:T(512)S(1)} %mul.754) | copy-start | bytes 6148
  95.9 20.4 %copy-start.64 = (f32[512]{0:T(512)S(1)}, f32[512]{0:T(512)}, u32[]{:S(2)}) copy-start(f32[512]{0:T(512)} %param.36) | copy-start | bytes 6148
  116.3 6.1 copy-start.95
  116.3 14.4 %copy-start.9 = (f32[1024,512]{1,0:T(8,128)S(1)}, f32[1024,512]{1,0:T(8,128)}, u32[]{:S(2)}) copy-start(f32[1024,512]{1,0:T(8,128)} %get-tuple-element.563) | copy-start | bytes 6291460
  139.8 5.8 copy-start.17
  185.7 7.1 %copy-start.4 = (f32[4,256,8,64]{1,3,2,0:T(8,128)S(1)}, f32[4,256,8,64]{1,3,2,0:T(8,128)}, u32[]{:S(2)}) copy-start(f32[4,256,8,64]{1,3,2,0:T(8,128)} %copy-done.3) | copy-start | bytes 6291460
  185.7 7.1 %copy-start.13 = (f32[1024,128]{1,0:T(8,128)S(1)}, f32[1024,128]{1,0:T(8,128)}, u32[]{:S(2)}) copy-start(f32[1024,128]{1,0:T(8,128)} %copy-done.12) | copy-start | bytes 1572868
  185.7 7.1 %copy-start.19 = (f32[4,8,128,64]{2,3,1,0:T(8,128)S(1)}, f32[4,8,128,64]{2,3,1,0:T(8,128)}, u32[]{:S(2)}) copy-start(f32[4,8,128,64]{2,3,1,0:T(8,128)} %get-tuple-element.321) | copy-start | bytes 3145732
  199.0 14.9 %copy-start.14 = (f32[1024,128]{1,0:T(8,128)S(1)}, f32[1024,128]{1,0:T(8,128)}, u32[]{:S(2)}) copy-start(f32[1024,128]{1,0:T(8,128)} %copy-done.12) | copy-start | bytes 1572868
  213.9 5.7 copy-start.46
  213.9 5.7 copy-start.52
  216.9 21.7 %copy-start.18 = (f32[4,256,8,64]{1,0,3,2:T(4,128)S(1)}, f32[4,256,8,64]{1,0,3,2:T(4,128)}, u32[]{:S(2)}) copy-start(f32[4,256,8,64]{1,0,3,2:T(4,128)} %get-tuple-element.875) | copy-start | bytes 6291460
  248.5 4.0 copy-start.20
  260.5 3.1 copy-start.10
  260.5 3.1 copy-start.67
  263.6 7.3 %copy-start.59 = (f32[1,512]{1,0:T(1,128)S(1)}, f32[1,512]{1,0:T(1,128)}, u32[]{:S(2)}) copy-start(f32[1,512]{1,0:T(1,128)} %copy-done.58) | copy-start | bytes 6148
  263.6 7.3 %copy-start.61 = (f32[1,512]{1,0:T(1,128)S(1)}, f32[1,512]{1,0:T(1,128)}, u32[]{:S(2)}) copy-start(f32[1,512]{1,0:T(1,128)} %copy-done.60) | copy-start | bytes 6148
  263.6 7.3 %copy-start.63 = (f32[1,512]{1,0:T(1,128)S(1)}, f32[1,512]{1,0:T(1,128)}, u32[]{:S(2)}) copy-start(f32[1,512]{1,0:T(1,128)} %copy-done.62) | copy-start | bytes 6148
  281.7 266.8 %reduce-scatter.2.cloned.1.call-start = ((), (), s32[]{:S(2)}) async-start(), calls=%async_computation.1 | async-start | bytes 5242880 | tf_op jit(solution)/shard_map/reduce_scatter | solution.py:151
  288.2 381.2 %all-reduce.33.cloned.1.call-start = ((), (), s32[]{:S(2)}) async-start(), calls=%async_computation.2 | async-start | bytes 14680064 | tf_op jit(solution)/shard_map/psum | solution.py:190
  289.7 3.9 copy-start.34
  470.4 3.9 copy-start.72
  470.4 3.9 copy-start.74
  470.4 4.0 copy-start.76
  479.7 3.5 copy-start.94
  482.1 3.1 copy-start.48
  482.1 3.1 copy-start.54
  485.2 5.6 copy-start.83
  485.2 31.8 %copy-start.68 = (f32[1024]{0:T(1024)S(1)}, f32[1024]{0:T(1024)}, u32[]{:S(2)}) copy-start(f32[1024]{0:T(1024)} %get-tuple-element.584) | copy-start | bytes 12292
  669.4 3.2 copy-start.30
  (55 other events, 108.8 us)
Sparse Core Ops, SparseCore 0:
  281.8 188.5 all-reduce.34
  472.7 75.7 reduce-scatter.1
  553.2 116.0 all-reduce.32
where the time goes:
time: 696 us; the launch traced here: 685 us
  waiting for transfers between devices  317 us (46%)
  matrix products  124 us (18%)
  local copies, waits for them, and re-layouts  93.4 us (13%)
  other arithmetic  87.7 us (13%)
  blocking collectives  48 us (7%)
  between operations  15.1 us (2%)
    psum x1, waiting for transfers between devices, per_device(): grad_normed = lax.psum(grad_local, 'tensor')  171 us
    psum x1, waiting for transfers between devices, per_device(): lax.psum((grad_norm_gain, grad_proj_gate, grad_proj_value, grad_proj_step...  118 us
    dot_general x3, matrix products, ssd_gate(): jnp.einsum('cijh,cjhp->cihp', weights, scaled, precision=HIGHEST)  35.6 us
    reduce_scatter x1, waiting for transfers between devices, per_device(): lax.psum_scatter(jnp.dot(gate_out, proj_out, preferred_element_type=jnp.f...  26.8 us
    psum x1, blocking collectives, per_device(): lax.psum((grad_norm_gain, grad_proj_gate, grad_proj_value, grad_proj_step...  26.2 us
    unnamed x196, local copies, waits for them, and re-layouts  20.6 us
    another operation x9, other arithmetic  16.7 us
  transfers between devices with their start and end apart: 3, of which 3 were waited for; matrix products, arithmetic and copies ran while one was open for 6% of the time, Pallas kernels for 0%

commit v1 on v0

v1 whole, which is shorter than its diff:
```python
from functools import partial

import jax
import jax.numpy as jnp
from jax import lax
from jax.experimental import pallas as pl
from jax.experimental.pallas import tpu as pltpu
from jax.sharding import PartitionSpec as P

EPS = 1e-05
HEAD = 64
NEG = -1e30
HI = lax.Precision.HIGHEST
F32 = jnp.float32
BF16 = jnp.bfloat16
NT = (((1,), (1,)), ((), ()))
TN = (((0,), (0,)), ((), ()))


def dot(a, b, dims=(((1,), (0,)), ((), ())), exact=False):
    return lax.dot_general(
        a, b, dims, precision=HI if exact else None, preferred_element_type=F32
    )


def iota(shape, axis):
    return lax.broadcasted_iota(jnp.int32, shape, axis)


def bounds_of(lens_ref, slots):
    ends, total = [], 0
    for s in range(slots):
        total = total + lens_ref[0, s]
        ends.append(total)
    return ends


def segment_of(position, ends):
    seg = jnp.zeros(position.shape, jnp.int32)
    for end in ends:
        seg = seg + (position >= end).astype(jnp.int32)
    return seg


def segment_at(position, ends):
    seg = jnp.int32(0)
    for end in ends:
        seg = seg + (position >= end).astype(jnp.int32)
    return seg


def sigmoid(v):
    return 1.0 / (1.0 + jnp.exp(-v))


def softplus(v):
    return jnp.maximum(v, 0.0) + jnp.log1p(jnp.exp(-jnp.abs(v)))


def spread(cols, heads):
    rows = cols.shape[0]
    low = iota((rows, 2 * HEAD), 1) < HEAD
    parts = []
    for h in range(0, heads, 2):
        a = jnp.broadcast_to(cols[:, h : h + 1], (rows, 2 * HEAD))
        b = jnp.broadcast_to(cols[:, h + 1 : h + 2], (rows, 2 * HEAD))
        parts.append(jnp.where(low, a, b))
    return jnp.concatenate(parts, axis=1)


def conv_pre(buf, block, rows, taps_ref, bias_ref, masks):
    count = taps_ref.shape[0]
    z = bias_ref[...] + taps_ref[count - 1 : count, :] * block
    for k in range(1, count):
        z = z + taps_ref[count - 1 - k : count - k, :] * (
            buf[pl.ds(8 - k, rows), :] * masks[k]
        )
    return z


def scan_terms(step_pre, step_bias, log_rate, ends, base, rows, heads):
    step_size = softplus(step_pre + step_bias)
    rate = -jnp.exp(log_rate)
    decay = step_size * rate
    tril = (iota((rows, rows), 0) >= iota((rows, rows), 1)).astype(F32)
    cum_col = dot(tril, decay, exact=True)
    cum_row = jnp.transpose(cum_col)
    col = segment_of(base + iota((rows, 1), 0), ends)
    row = segment_of(base + iota((1, rows), 1), ends)
    seg_last = segment_at(base + rows - 1, ends)
    seg_before = jnp.where(base > 0, segment_at(base - 1, ends), -1)
    cum_end = cum_col[rows - 1 : rows, :]
    carry_in = jnp.exp(cum_col) * (col == seg_before).astype(F32)
    to_end = jnp.exp(cum_end - cum_col) * (col == seg_last).astype(F32)
    passes = jnp.exp(cum_end) * (seg_last == seg_before).astype(F32)
    return step_size, rate, cum_col, cum_row, col, row, carry_in, to_end, passes


def conv_masks(base, rows, taps, ends, col):
    position = base + iota((rows, 1), 0)
    masks = [None]
    for k in range(1, taps):
        before = segment_of(position - k, ends)
        masks.append(((before == col) & (position >= k)).astype(F32))
    return masks


def forward_kernel(
    lens_ref, tok_ref, cot_ref, gain_ref, wg_ref, wv_ref, wp_ref, ws_ref,
    cv_ref, cvb_ref, cp_ref, cpb_ref, sb_ref, lr_ref, sg_ref, gg_ref, wo_ref,
    normed_ref, gate_ref, value_ref, pair_ref, step_ref, ssd_ref, ggo_ref,
    states_ref, mixed_ref, stats_ref,
    vbuf, pbuf, state,
):
    b = pl.program_id(0)
    rows = tok_ref.shape[0]
    heads = ws_ref.shape[1]
    n = pair_ref.shape[1] // 2
    base = b * rows

    @pl.when(b == 0)
    def _():
        vbuf[0:8, :] = jnp.zeros((8, vbuf.shape[1]), F32)
        pbuf[0:8, :] = jnp.zeros((8, pbuf.shape[1]), F32)
        state[...] = jnp.zeros_like(state)

    ends = bounds_of(lens_ref, lens_ref.shape[1])
    tok = tok_ref[...].astype(F32)
    scale_in = lax.rsqrt(jnp.mean(tok * tok, axis=1, keepdims=True) + EPS)
    normed = (tok * scale_in * gain_ref[...]).astype(BF16)
    normed_ref[...] = normed
    gate_pre = dot(normed, wg_ref[...])
    gate_ref[...] = gate_pre
    value_pre = dot(normed, wv_ref[...])
    value_ref[...] = value_pre
    pair_pre = dot(normed, wp_ref[...])
    pair_ref[...] = pair_pre
    step_pre = dot(normed, ws_ref[...])
    step_ref[...] = step_pre
    vbuf[8:, :] = value_pre
    pbuf[8:, :] = pair_pre

    step_size, rate, cum_col, cum_row, col, row, carry_in, to_end, passes = scan_terms(
        step_pre, sb_ref[...], lr_ref[...], ends, base, rows, heads
    )
    masks = conv_masks(base, rows, cv_ref.shape[0], ends, col)
    zv = conv_pre(vbuf, value_pre, rows, cv_ref, cvb_ref, masks)
    value = zv * sigmoid(zv)
    zp = conv_pre(pbuf, pair_pre, rows, cp_ref, cpb_ref, masks)
    pair = zp * sigmoid(zp)
    vbuf[0:8, :] = vbuf[rows : rows + 8, :]
    pbuf[0:8, :] = pbuf[rows : rows + 8, :]
    b_rows, c_rows = pair[:, :n], pair[:, n:]

    scaled = value * spread(step_size, heads)
    low_scaled = scaled.astype(BF16)
    scores = dot(c_rows, b_rows, NT, exact=True)
    causal = iota((rows, rows), 0) >= iota((rows, rows), 1)
    bar = jnp.where(causal & (col == row), 0.0, NEG)
    low = iota((rows, 2 * HEAD), 1) < HEAD
    parts = []
    for h in range(0, heads, 2):
        lanes = low_scaled[:, h * HEAD : (h + 2) * HEAD]
        outs = []
        for g in (h, h + 1):
            gap = cum_col[:, g : g + 1] - cum_row[g : g + 1, :]
            weights = (scores * jnp.exp(gap + bar)).astype(BF16)
            outs.append(dot(weights, lanes))
        parts.append(jnp.where(low, outs[0], outs[1]))
    prev = state[...]
    states_ref[0] = prev
    ssd = jnp.concatenate(parts, axis=1) + spread(carry_in, heads) * dot(
        c_rows, prev, exact=True
    )
    state[...] = spread(passes, heads) * prev + dot(
        b_rows, low_scaled.astype(F32) * spread(to_end, heads), TN, exact=True
    )
    ssd = ssd + spread(sg_ref[...], heads) * value
    ssd_ref[...] = ssd

    gated = ssd * (gate_pre * sigmoid(gate_pre))
    weighed = gated * gg_ref[...]
    mixed_ref[...] = dot(weighed.astype(BF16), wo_ref[...])
    live = base + iota((rows, 1), 0) < ends[-1]
    cot = jnp.where(live, cot_ref[...].astype(F32), 0.0).astype(BF16)
    ggo = dot(cot, wo_ref[...], NT)
    ggo_ref[...] = ggo
    ones = jnp.ones((8, gated.shape[1]), F32)
    square = dot(ones, gated * gated, NT, exact=True)
    stat = dot(ones, ggo * weighed, NT, exact=True)
    stats_ref[...] = jnp.concatenate([square[0:1, :], stat[0:1, :]], axis=0)


def backward_kernel(
    lens_ref, stats_ref, gate_ref, value_ref, vprev_ref, pair_ref, pprev_ref,
    step_ref, ssd_ref, ggo_ref, states_ref,
    wg_ref, wv_ref, wp_ref, ws_ref,
    cv_ref, cvb_ref, cp_ref, cpb_ref, sb_ref, lr_ref, sg_ref, gg_ref,
    gate_out_ref, lowg_ref, lowv_ref, lowp_ref, lows_ref, grad_ref, scale_ref,
    ggg_ref, gcv_ref, gcvb_ref, gcp_ref, gcpb_ref, gsb_ref, glr_ref, gsg_ref,
    vbuf, pbuf, dvbuf, dpbuf, dstate, dcarry,
    *, channels,
):
    i = pl.program_id(0)
    blocks = pl.num_programs(0)
    b = blocks - 1 - i
    rows = gate_ref.shape[0]
    heads = ws_ref.shape[1]
    n = pair_ref.shape[1] // 2
    taps = cv_ref.shape[0]
    base = b * rows

    @pl.when(i == 0)
    def _():
        dvbuf[rows:, :] = jnp.zeros((8, dvbuf.shape[1]), F32)
        dpbuf[rows:, :] = jnp.zeros((8, dpbuf.shape[1]), F32)
        dstate[...] = jnp.zeros_like(dstate)
        dcarry[...] = jnp.zeros_like(dcarry)
        for ref in (ggg_ref, gcv_ref, gcvb_ref, gcp_ref, gcpb_ref, gsb_ref, glr_ref, gsg_ref):
            ref[...] = jnp.zeros_like(ref)

    ends = bounds_of(lens_ref, lens_ref.shape[1])
    eye = (iota((rows, rows), 0) == iota((rows, rows), 1)).astype(F32)
    stats = dot(eye, stats_ref[...], NT, exact=True)
    scale = lax.rsqrt(stats[:, 0:1] / channels + EPS)
    scale_ref[...] = scale
    pull = scale * scale * scale / channels * stats[:, 1:2]

    gate_pre = gate_ref[...]
    sig_gate = sigmoid(gate_pre)
    silu_gate = gate_pre * sig_gate
    ssd = ssd_ref[...]
    ggo = ggo_ref[...]
    gated = ssd * silu_gate
    scaled_gated = gated * scale
    gate_out_ref[...] = (scaled_gated * gg_ref[...]).astype(BF16)
    ggg_ref[...] += jnp.sum(ggo * scaled_gated, axis=0, keepdims=True)
    grad_gated = ggo * gg_ref[...] * scale - gated * pull
    low_gate = (grad_gated * ssd * (sig_gate * (1.0 + gate_pre * (1.0 - sig_gate)))).astype(BF16)
    lowg_ref[...] = low_gate
    grad_ssd = grad_gated * silu_gate

    step_pre = step_ref[...]
    step_size, rate, cum_col, cum_row, col, row, carry_in, to_end, passes = scan_terms(
        step_pre, sb_ref[...], lr_ref[...], ends, base, rows, heads
    )
    masks = conv_masks(base, rows, taps, ends, col)
    value_pre, pair_pre = value_ref[...], pair_ref[...]
    vbuf[0:8, :] = vprev_ref[...]
    pbuf[0:8, :] = pprev_ref[...]
    vbuf[8:, :] = value_pre
    pbuf[8:, :] = pair_pre
    zv = conv_pre(vbuf, value_pre, rows, cv_ref, cvb_ref, masks)
    sig_v = sigmoid(zv)
    value = zv * sig_v
    zp = conv_pre(pbuf, pair_pre, rows, cp_ref, cpb_ref, masks)
    sig_p = sigmoid(zp)
    pair = zp * sig_p
    b_rows, c_rows = pair[:, :n], pair[:, n:]

    step_wide = spread(step_size, heads)
    scaled = value * step_wide
    low_scaled = scaled.astype(BF16)
    low_grad = grad_ssd.astype(BF16)
    round_scaled = low_scaled.astype(F32)
    round_grad = low_grad.astype(F32)
    skip = spread(sg_ref[...], heads)
    gsg_ref[...] += jnp.sum(grad_ssd * value, axis=0, keepdims=True)

    scores_t = dot(b_rows, c_rows, NT, exact=True)
    causal_t = iota((rows, rows), 0) <= iota((rows, rows), 1)
    bar_t = jnp.where(causal_t & (col == row), 0.0, NEG)
    low = iota((rows, 2 * HEAD), 1) < HEAD
    zero = jnp.zeros((rows, 2 * HEAD), BF16)
    grad_scores_t = jnp.zeros((rows, rows), F32)
    parts = []
    for h in range(0, heads, 2):
        own = slice(h * HEAD, (h + 2) * HEAD)
        lanes_x, lanes_y = low_scaled[:, own], low_grad[:, own]
        outs = []
        for g in (h, h + 1):
            gap = cum_row[g : g + 1, :] - cum_col[:, g : g + 1]
            fall = jnp.exp(gap + bar_t)
            weights = (scores_t * fall).astype(BF16)
            outs.append(dot(weights, lanes_y))
            half = jnp.where(low, lanes_x, zero) if g == h else jnp.where(low, zero, lanes_x)
            grad_scores_t += dot(half, lanes_y, NT) * fall
        parts.append(jnp.where(low, outs[0], outs[1]))
    prev, later = states_ref[0], dstate[...]
    end_wide = spread(to_end, heads)
    carry_grad = round_grad * spread(carry_in, heads)
    grad_scaled = jnp.concatenate(parts, axis=1) + end_wide * dot(b_rows, later, exact=True)
    grad_c = dot(grad_scores_t, b_rows, TN, exact=True) + dot(carry_grad, prev, NT, exact=True)
    grad_b = dot(grad_scores_t, c_rows, exact=True) + dot(
        round_scaled * end_wide, later, NT, exact=True
    )
    dstate[...] = spread(passes, heads) * later + dot(c_rows, carry_grad, TN, exact=True)

    heads_of = (iota((scaled.shape[1], heads), 0) // HEAD == iota((scaled.shape[1], heads), 1)).astype(F32)
    inner = ssd - skip * value
    grad_cum = dot(round_grad * inner - round_scaled * grad_scaled, heads_of, exact=True)
    grad_step = dot(value * grad_scaled, heads_of, exact=True)
    seg_last = segment_at(base + rows - 1, ends)
    seg_after = segment_at(base + rows, ends)
    suffix = (causal_t & (col == row)).astype(F32)
    grad_decay = dot(suffix, grad_cum, exact=True) + dcarry[...] * (
        (col == seg_last) & (seg_last == seg_after)
    ).astype(F32)
    dcarry[...] = grad_decay[0:1, :]
    grad_step = grad_step + grad_decay * rate
    glr_ref[...] += rate * jnp.sum(grad_decay * step_size, axis=0, keepdims=True)
    grad_step_pre = grad_step * sigmoid(step_pre + sb_ref[...])
    gsb_ref[...] += jnp.sum(grad_step_pre, axis=0, keepdims=True)
    low_step = grad_step_pre.astype(BF16)
    lows_ref[...] = low_step

    position = base + iota((rows, 1), 0)
    total = blocks * rows
    after = [None]
    for k in range(1, taps):
        after.append(((segment_of(position + k, ends) == col) & (position + k < total)).astype(F32))

    def conv_back(grad_post, z, sig, block, buf, dbuf, taps_ref, gtaps_ref, gbias_ref):
        dz = grad_post * (sig * (1.0 + z * (1.0 - sig)))
        dbuf[0:rows, :] = dz
        gbias_ref[...] += jnp.sum(dz, axis=0, keepdims=True)
        gtaps_ref[taps - 1 : taps, :] += jnp.sum(dz * block, axis=0, keepdims=True)
        pre = taps_ref[taps - 1 : taps, :] * dz
        for k in range(1, taps):
            gtaps_ref[taps - 1 - k : taps - k, :] += jnp.sum(
                dz * (buf[pl.ds(8 - k, rows), :] * masks[k]), axis=0, keepdims=True
            )
            pre = pre + taps_ref[taps - 1 - k : taps - k, :] * (
                dbuf[pl.ds(k, rows), :] * after[k]
            )
        dbuf[rows:, :] = dz[0:8, :]
        return pre

    grad_value = skip * grad_ssd + step_wide * grad_scaled
    low_value = conv_back(
        grad_value, zv, sig_v, value_pre, vbuf, dvbuf, cv_ref, gcv_ref, gcvb_ref
    ).astype(BF16)
    lowv_ref[...] = low_value
    low_pair = conv_back(
        jnp.concatenate([grad_b, grad_c], axis=1), zp, sig_p, pair_pre, pbuf, dpbuf,
        cp_ref, gcp_ref, gcpb_ref,
    ).astype(BF16)
    lowp_ref[...] = low_pair
    grad_ref[...] = (
        dot(low_gate, wg_ref[...], NT)
        + dot(low_value, wv_ref[...], NT)
        + dot(low_pair, wp_ref[...], NT)
        + dot(low_step, ws_ref[...], NT)
    )


def params():
    return pltpu.CompilerParams(
        dimension_semantics=("arbitrary",), vmem_limit_bytes=60 * 1024 * 1024
    )


def forward_call(lens, tokens, cotangent, whole, sizes):
    rows, width, group, channels, heads, pair = sizes
    blocks = rows // group
    n = pair // 2
    rowed = lambda w: pl.BlockSpec((group, w), lambda i: (i, 0))
    fixed = lambda a: pl.BlockSpec(a.shape, lambda i: (0,) * a.ndim)
    shape = jax.ShapeDtypeStruct
    return pl.pallas_call(
        forward_kernel,
        grid=(blocks,),
        in_specs=[
            pl.BlockSpec(memory_space=pltpu.SMEM),
            rowed(width),
            rowed(width),
            *[fixed(a) for a in whole],
        ],
        out_specs=[
            rowed(width), rowed(channels), rowed(channels), rowed(pair), rowed(heads),
            rowed(channels), rowed(channels),
            pl.BlockSpec((1, n, channels), lambda i: (i, 0, 0)),
            rowed(width),
            pl.BlockSpec((2, group), lambda i: (0, i)),
        ],
        out_shape=[
            shape((rows, width), BF16),
            shape((rows, channels), F32),
            shape((rows, channels), F32),
            shape((rows, pair), F32),
            shape((rows, heads), F32),
            shape((rows, channels), F32),
            shape((rows, channels), F32),
            shape((blocks, n, channels), F32),
            shape((rows, width), F32),
            shape((2, rows), F32),
        ],
        scratch_shapes=[
            pltpu.VMEM((group + 8, channels), F32),
            pltpu.VMEM((group + 8, pair), F32),
            pltpu.VMEM((n, channels), F32),
        ],
        compiler_params=params(),
        name="fwd",
    )(lens, tokens, cotangent, *whole)


def backward_call(lens, stats, saved, weights, small, sizes, full_channels):
    rows, width, group, channels, heads, pair = sizes
    blocks = rows // group
    n = pair // 2
    per = group // 8
    gate_pre, value_pre, pair_pre, step_pre, ssd, ggo, states = saved
    back = lambda w: pl.BlockSpec((group, w), lambda i: (blocks - 1 - i, 0))
    above = lambda w: pl.BlockSpec(
        (8, w), lambda i: (jnp.maximum((blocks - 1 - i) * per - 1, 0), 0)
    )
    fixed = lambda a: pl.BlockSpec(a.shape, lambda i: (0,) * a.ndim)
    total = lambda r, w: pl.BlockSpec((r, w), lambda i: (0, 0))
    shape = jax.ShapeDtypeStruct
    taps = small[0].shape[0]
    sums = [
        (1, channels), (taps, channels), (1, channels), (taps, pair), (1, pair),
        (1, heads), (1, heads), (1, channels),
    ]
    return pl.pallas_call(
        partial(backward_kernel, channels=full_channels),
        grid=(blocks,),
        in_specs=[
            pl.BlockSpec(memory_space=pltpu.SMEM),
            pl.BlockSpec((2, group), lambda i: (0, blocks - 1 - i)),
            back(channels), back(channels), above(channels), back(pair), above(pair),
            back(heads), back(channels), back(channels),
            pl.BlockSpec((1, n, channels), lambda i: (blocks - 1 - i, 0, 0)),
            *[fixed(a) for a in weights],
            *[fixed(a) for a in small],
        ],
        out_specs=[
            back(channels), back(channels), back(channels), back(pair), back(heads),
            back(width), back(1),
            *[total(*s) for s in sums],
        ],
        out_shape=[
            shape((rows, channels), BF16),
            shape((rows, channels), BF16),
            shape((rows, channels), BF16),
            shape((rows, pair), BF16),
            shape((rows, heads), BF16),
            shape((rows, width), F32),
            shape((rows, 1), F32),
            *[shape(s, F32) for s in sums],
        ],
        scratch_shapes=[
            pltpu.VMEM((group + 8, channels), F32),
            pltpu.VMEM((group + 8, pair), F32),
            pltpu.VMEM((group + 8, channels), F32),
            pltpu.VMEM((group + 8, pair), F32),
            pltpu.VMEM((n, channels), F32),
            pltpu.VMEM((1, heads), F32),
        ],
        compiler_params=params(),
        name="bwd",
    )(
        lens, stats, gate_pre, value_pre, value_pre, pair_pre, pair_pre, step_pre, ssd,
        ggo, states, *weights, *small,
    )


def per_device(
    tokens, cotangent, seq_lengths, norm_gain, proj_gate, proj_value, proj_pair,
    proj_step, conv_value, conv_value_bias, conv_pair, conv_pair_bias, step_bias,
    log_rate, skip_gain, gate_gain, proj_out,
):
    rows, width = tokens.shape
    channels, heads, pair = proj_gate.shape[1], proj_step.shape[1], proj_pair.shape[1]
    ways = lax.axis_size("tensor")
    full_channels = channels * ways
    group = min(256, rows)
    sizes = (rows, width, group, channels, heads, pair)
    line = lambda a: a[None, :]
    small = (
        conv_value, line(conv_value_bias), conv_pair, line(conv_pair_bias),
        line(step_bias), line(log_rate), line(skip_gain), line(gate_gain),
    )
    weights = (proj_gate, proj_value, proj_pair, proj_step)
    normed, gate_pre, value_pre, pair_pre, step_pre, ssd, ggo, states, mixed, stats = (
        forward_call(
            seq_lengths, tokens, cotangent,
            (line(norm_gain), *weights, *small, proj_out), sizes,
        )
    )
    stats = lax.psum(stats, "tensor")
    mixed_rows = lax.psum_scatter(mixed, "tensor", scatter_dimension=0, tiled=True)
    (
        gate_out, low_gate, low_value, low_pair, low_step, grad_local, scale,
        g_gain, g_cv, g_cvb, g_cp, g_cpb, g_sb, g_lr, g_sg,
    ) = backward_call(
        seq_lengths, stats, (gate_pre, value_pre, pair_pre, step_pre, ssd, ggo, states),
        weights, small, sizes, full_channels,
    )

    share = rows // ways
    first = lax.axis_index("tensor") * share
    own = lambda a: lax.dynamic_slice_in_dim(a, first, share, 0)
    grad_normed = lax.psum_scatter(grad_local, "tensor", scatter_dimension=0, tiled=True)
    own_tok = own(tokens).astype(F32)
    scale_in = lax.rsqrt(jnp.mean(own_tok * own_tok, axis=1, keepdims=True) + EPS)
    g_norm = jnp.sum(grad_normed * own_tok * scale_in, axis=0)
    scaled_grad = grad_normed * norm_gain[None, :]
    row_dot = jnp.sum(scaled_grad * own_tok, axis=1, keepdims=True)
    grad_wide = scaled_grad * scale_in - own_tok * (scale_in**3 / width) * row_dot
    grad_wide = lax.all_gather(grad_wide, "tensor", axis=0, tiled=True)
    grad_tokens = (cotangent.astype(F32) + grad_wide).astype(BF16)

    live = jnp.arange(rows, dtype=jnp.int32) < jnp.sum(seq_lengths)
    block_out = (
        own_tok + jnp.where(own(live)[:, None], mixed_rows * own(scale), 0.0)
    ).astype(BF16)

    cot_live = jnp.where(live[:, None], cotangent, jnp.zeros_like(cotangent))
    tn = lambda a, b: lax.dot_general(a, b, TN, preferred_element_type=F32)
    g_out = tn(gate_out, cot_live)
    g_gate = tn(normed, low_gate)
    g_value = tn(normed, low_value)
    g_pair = tn(normed, low_pair)
    g_step = tn(normed, low_step)
    g_skip = jnp.sum(g_sg.reshape(heads, HEAD), axis=1)
    g_out, g_gate, g_value = lax.psum((g_out, g_gate, g_value), "dp")
    g_step, g_cv, g_cvb, g_sb, g_lr, g_skip, g_gain = lax.psum(
        (g_step, g_cv, g_cvb[0], g_sb[0], g_lr[0], g_skip, g_gain[0]), "dp"
    )
    g_pair, g_cp, g_cpb, g_norm = lax.psum((g_pair, g_cp, g_cpb[0], g_norm), ("dp", "tensor"))
    return (
        block_out, grad_tokens, g_norm, g_gate, g_value, g_pair, g_step, g_cv, g_cvb,
        g_cp, g_cpb, g_sb, g_lr, g_skip, g_gain, g_out,
    )


def solution(mesh):
    return jax.shard_map(
        per_device,
        mesh=mesh,
        in_specs=(
            P("dp", None),
            P("dp", None),
            P("dp", None),
            P(),
            P(None, "tensor"),
            P(None, "tensor"),
            P(),
            P(None, "tensor"),
            P(None, "tensor"),
            P("tensor"),
            P(),
            P(),
            P("tensor"),
            P("tensor"),
            P("tensor"),
            P("tensor"),
            P("tensor", None),
        ),
        out_specs=(
            P(("dp", "tensor"), None),
            P("dp", None),
            P(),
            P(None, "tensor"),
            P(None, "tensor"),
            P(),
            P(None, "tensor"),
            P(None, "tensor"),
            P("tensor"),
            P(),
            P(),
            P("tensor"),
            P("tensor"),
            P("tensor"),
            P("tensor"),
            P("tensor", None),
        ),
        check_vma=False,
    )
```

time: 696 us -> 568 us (0.82); the launches traced: 685 us -> 568 us
  matrix products: 124 us -> 13.5 us
  local copies, waits for them, and re-layouts: 93.4 us -> 11.9 us
  other arithmetic: 87.7 us -> 11 us
  Pallas kernels: 0 us -> 64.9 us
  waiting for transfers between devices: 317 us -> 367 us
  blocking collectives: 48 us -> 84 us
    reduce_scatter x1 -> x2, waiting for transfers between devices: 26.8 us -> 150 us  [the longest x1 78 us: per_device(): lax.psum_scatter(mixed, 'tensor', scatter_dimension=0, tiled=True)]
    dot_general x32 -> x5, matrix products: 118 us -> 13.5 us  [per_device(): tn = lambda a, b: lax.dot_general(a, b, TN, preferred_element_type=F32)]
    psum x2, waiting for transfers between devices: 290 us -> 216 us  [the longest x1 109 us: per_device(): lax.psum((g_pair, g_cp, g_cpb[0], g_norm), ('dp', 'tensor'))]
    pallas_call x0 -> x2, Pallas kernels: none -> 64.9 us  [the longest x1 38.7 us: backward_call(): pl.pallas_call(partial(backward_kernel, channels=full_channels), grid=(bl...]
    psum x3, blocking collectives: 48 us -> 84 us  [the longest x1 43 us: per_device(): lax.psum((g_pair, g_cp, g_cpb[0], g_norm), ('dp', 'tensor'))]
    reshape x10 -> x1, local copies, waits for them, and re-layouts: 29.4 us -> 0.08 us  [per_device(): g_skip = jnp.sum(g_sg.reshape(heads, HEAD), axis=1)]
    reduce_sum x17 -> x4, other arithmetic: 26.2 us -> 2.59 us  [the longest x1 1.64 us: per_device(): g_norm = jnp.sum(grad_normed * own_tok * scale_in, axis=0)]
    another operation x9 -> x0, other arithmetic: 16.7 us -> none
  transfers between devices with their start and end apart: 3 -> 5, of which waited for: 3 -> 4; matrix products, arithmetic and copies ran while one was open for 6% -> 4% of each run, Pallas kernels for 0% -> 0%
where the time goes in v1:
time: 568 us
  waiting for transfers between devices  367 us (65%)
  blocking collectives  84 us (15%)
  Pallas kernels  64.9 us (11%)
  between operations  15.4 us (3%)
  matrix products  13.5 us (2%)
  local copies, waits for them, and re-layouts  11.9 us (2%)
  other arithmetic  11 us (2%)
    psum x1, waiting for transfers between devices, per_device(): lax.psum((g_pair, g_cp, g_cpb[0], g_norm), ('dp', 'tensor'))  109 us
    psum x1, waiting for transfers between devices, per_device(): g_out, g_gate, g_value = lax.psum((g_out, g_gate, g_value), 'dp')  107 us
    reduce_scatter x1, waiting for transfers between devices, per_device(): lax.psum_scatter(mixed, 'tensor', scatter_dimension=0, tiled=True)  78 us
    reduce_scatter x1, waiting for transfers between devices, per_device(): lax.psum_scatter(grad_local, 'tensor', scatter_dimension=0, tiled=True)  71.8 us
    psum x1, blocking collectives, per_device(): lax.psum((g_pair, g_cp, g_cpb[0], g_norm), ('dp', 'tensor'))  43 us
    pallas_call x1, Pallas kernels, backward_call(): pl.pallas_call(partial(backward_kernel, channels=full_channels), grid=(bl...  38.7 us
    psum x1, blocking collectives, per_device(): lax.psum((g_step, g_cv, g_cvb[0], g_sb[0], g_lr[0], g_skip, g_gain[0]), '...  26.3 us
    pallas_call x1, Pallas kernels, forward_call(): pl.pallas_call(forward_kernel, grid=(blocks,), in_specs=[pl.BlockSpec(mem...  26.2 us
  transfers between devices with their start and end apart: 5, of which 4 were waited for; matrix products, arithmetic and copies ran while one was open for 4% of the time, Pallas kernels for 0%

profile of v1, /device:TPU:0, one launch (start us, length us, event | category | flops | bytes accessed | tf_op | source)
XLA Modules:
  0.0 567.8 jit_solution(6841792191139162533)
XLA Ops:
  8.0 0.0 reduce-scatter.5.cloned.1.call-start
  8.1 1.5 copy.35.ws_ref
  9.6 26.2 %fwd.1 = (bf16[1024,1024]{1,0:T(8,128)(2,1)}, f32[1024,512]{1,0:T(8,128)}, f32[1024,512]{1,0:T(8,128)}, f32[1024,256]{1,0:T(8,128)}, f32[1024,8]{1,0:T(8,128)}, ...) custom-call(s32[1,8]{1,0:T(1,128)} %lens_ref.3, ...), custom_call_target="tpu_custom_call" | custom-call | tf_op jit(solution)/shard_map/fwd/pallas_call | solution.py:370
  35.8 14.6 %psum.105.stats_ref = f32[2,1024]{1,0:T(2,128)} all-reduce(f32[2,1024]{1,0:T(2,128)} %get-tuple-element.42), channel_id=1, replica_groups=mesh['dp'=8,'tensor'=4] {'tensor'}, use_global_device_ids=true, to_apply=%region_2.0 | all-reduce | flops 2048 | bytes 16384 | tf_op jit(solution)/shard_map/psum | solution.py:492
  50.4 38.7 %bwd.1 = (bf16[1024,512]{1,0:T(8,128)(2,1)}, bf16[1024,512]{1,0:T(8,128)(2,1)}, bf16[1024,512]{1,0:T(8,128)(2,1)}, bf16[1024,256]{1,0:T(8,128)(2,1)}, bf16[1024,...) custom-call(s32[1,8]{1,0:T(1,128)} %lens_ref.3, ...), custom_call_target="tpu_custom_call" | custom-call | tf_op jit(solution)/shard_map/bwd/pallas_call | solution.py:426
  89.1 0.0 reduce-scatter.5.cloned.1.call-update
  89.1 0.0 reduce-scatter.3.cloned.1.call-start
  89.2 0.0 copy-start.12
  89.2 0.0 copy-start.1
  89.2 0.7 reduce-scatter.3.cloned.1.call-update
  89.9 0.0 all-gather.2.cloned.1.call-start
  89.9 0.6 reduce_sum.45
  90.6 0.6 iota_compare_fusion
  91.2 0.1 dynamic_slice.10
  91.3 1.0 dynamic-slice_reduce_fusion
  92.3 0.2 fusion.4
  92.5 71.8 %reduce-scatter.5.cloned.1.call-done = f32[256,1024]{1,0:T(8,128)} async-done(((f32[1024,1024]{1,0:T(8,128)}), f32[256,1024]{1,0:T(8,128)}) %reduce-scatter.5.cloned.1.call-update) | async-done | bytes 1048592 | tf_op jit(solution)/shard_map/reduce_scatter | solution.py:505
  164.3 1.6 fusion.9
  166.0 78.0 %reduce-scatter.3.cloned.1.call-done = f32[256,1024]{1,0:T(8,128)} async-done(((f32[1024,1024]{1,0:T(8,128)}), f32[256,1024]{1,0:T(8,128)}) %reduce-scatter.3.cloned.1.call-update) | async-done | bytes 1048592 | tf_op jit(solution)/shard_map/reduce_scatter | solution.py:493
  243.9 2.8 fusion.6
  246.7 0.0 all-gather.2.cloned.1.call-update
  246.7 0.0 all-reduce.6.cloned.1.call-start
  246.8 0.0 copy-start.3
  246.8 3.7 fusion.15
  250.5 0.0 all-reduce.6.cloned.1.call-update
  250.5 0.3 all-reduce.8.cloned.1.call-start
  250.8 2.6 fusion.13
  253.4 2.6 fusion.14
  256.0 2.7 fusion
  258.7 0.0 all-reduce.8.cloned.1.call-update
  258.7 0.0 copy-start.10
  258.8 0.5 broadcast.42
  259.3 0.1 copy-done.15
  259.4 0.7 reduce.5
  260.0 0.1 reshape.58
  260.1 0.1 reduce_sum.49
  260.2 2.0 fusion.16
  262.3 26.3 %all-reduce.1 = (f32[1024,8]{0,1:T(8,128)}, f32[4,512]{1,0:T(4,128)}, f32[512]{0:T(512)}, f32[8]{0:T(128)}, f32[8]{0:T(128)}, /*index=5*/f32[8]{0:T(128)}, f32[512]{0:T(512)}) all-reduce(f32[1024,8]{0,1:T(8,128)S(1)} %fusion.16, f32[4,512]{1,0:T(4,128)S(1)} %copy-done.10, ...), channel_id=1, replica_groups=mesh['dp'=8,'tensor'=4] {'dp'}, use_global_device_ids=true, to_apply=%region_11.12 | all-reduce | flops 11288 | bytes 90304 | tf_op jit(solution)/shard_map/psum | solution.py:529
  288.6 43.0 %all-reduce = (f32[1024]{0:T(1024)}, f32[4,256]{1,0:T(4,128)}, f32[256]{0:T(256)}) all-reduce(f32[1024]{0:T(1024)S(1)} %get-tuple-element.66, f32[4,256]{1,0:T(4,128)S(1)} %copy-done.11, f32[256]{0:T(256)S(1)} %bitcast.36), channel_id=1, replica_groups=mesh['dp'=8,'tensor'=4] {'dp','tensor'}, use_global_device_ids=true, to_apply=%region_7.8 | all-reduce | flops 2304 | bytes 18432 | tf_op jit(solution)/shard_map/psum | solution.py:532
  331.6 4.4 add_convert_fusion
  336.0 109.4 %all-reduce.6.cloned.1.call-done = f32[1024,256]{1,0:T(8,128)} async-done(((f32[1024,256]{1,0:T(8,128)}), f32[1024,256]{1,0:T(8,128)}) %all-reduce.6.cloned.1.call-update) | async-done | bytes 1048592 | tf_op jit(solution)/shard_map/psum | solution.py:532
  445.4 106.8 %all-reduce.8.cloned.1.call-done = (f32[1024,512]{1,0:T(8,128)}, f32[1024,512]{1,0:T(8,128)}, f32[512,1024]{1,0:T(8,128)}) async-done(((f32[1024,512]{1,0:T(8,128)}, f32[1024,512]{1,0:T(8,128)}, f32[512,1024]{1,0:T(8,128)}), (f32[1024,512]{1,0:T(8,128)}, f32[1024,512]{1,0:T(8,128)}, f32[512,1024]{1,0:T(8,128)})) %all-reduce.8.cloned.1.call-update) | async-done | bytes 6291472 | tf_op jit(solution)/shard_map/psum | solution.py:528
  552.2 3.2 copy.41
  555.4 1.3 copy.42
  556.7 0.6 copy-done.7
  557.4 1.0 copy.43
  558.3 1.0 copy-done.5
  559.3 1.3 copy.44
  (39 shorter events, 0.1 us)
Async XLA Ops:
  8.0 156.3 %reduce-scatter.5.cloned.1.call-start = ((), (), s32[]{:S(2)}) async-start(), calls=%async_computation.3 | async-start | bytes 5242880 | tf_op jit(solution)/shard_map/reduce_scatter | solution.py:505
  89.1 154.8 %reduce-scatter.3.cloned.1.call-start = ((), (), s32[]{:S(2)}) async-start(), calls=%async_computation.2 | async-start | bytes 5242880 | tf_op jit(solution)/shard_map/reduce_scatter | solution.py:493
  89.2 0.8 copy-start.12
  89.2 3.1 copy-start.1
  89.2 75.1 %copy-start.9 = (f32[1024]{0:T(1024)S(1)}, f32[1024]{0:T(1024)}, u32[]{:S(2)}) copy-start(f32[1024]{0:T(1024)} %param.20) | copy-start | bytes 12292
  89.9 241.8 %all-gather.2.cloned.1.call-start = ((), (), s32[]{:S(2)}) async-start(), calls=%async_computation.4 | async-start | bytes 5242880 | tf_op jit(solution)/shard_map/all_gather | solution.py:512
  164.3 79.6 %copy-start.2 = (f32[256,1024]{1,0:T(8,128)S(1)}, f32[256,1024]{1,0:T(8,128)}, u32[]{:S(2)}) copy-start(f32[256,1024]{1,0:T(8,128)} %reduce-scatter.5.cloned.1.call-done) | copy-start | bytes 3145732
  246.7 198.7 %all-reduce.6.cloned.1.call-start = ((), (), s32[]{:S(2)}) async-start(), calls=%async_computation.5 | async-start | bytes 2097152 | tf_op jit(solution)/shard_map/psum | solution.py:532
  246.8 4.0 copy-start.3
  246.8 4.0 copy-start.21
  250.5 301.7 %all-reduce.8.cloned.1.call-start = ((), (), s32[]{:S(2)}) async-start(), calls=%async_computation.6 | async-start | bytes 12582912 | tf_op jit(solution)/shard_map/psum | solution.py:528
  250.8 2.6 copy-start.4
  250.8 2.6 copy-start.20
  253.4 2.6 copy-start
  253.4 2.6 copy-start.19
  258.7 0.7 copy-start.15
  258.7 1.5 copy-start.8
  258.7 3.5 copy-start.10
  258.7 3.5 copy-start.13
  258.7 3.5 copy-start.14
  258.7 3.5 copy-start.17
  258.7 3.5 copy-start.18
  258.8 29.9 %copy-start.11 = (f32[4,256]{1,0:T(4,128)S(1)}, f32[4,256]{1,0:T(4,128)}, u32[]{:S(2)}) copy-start(f32[4,256]{1,0:T(4,128)} %get-tuple-element.59) | copy-start | bytes 12292
  258.8 29.8 %copy-start.16 = (f32[1,256]{1,0:T(1,128)S(1)}, f32[1,256]{1,0:T(1,128)}, u32[]{:S(2)}) copy-start(f32[1,256]{1,0:T(1,128)} %get-tuple-element.60) | copy-start | bytes 3076
  552.2 3.2 copy-start.6
  555.4 2.0 copy-start.7
  557.4 2.0 copy-start.5
Sparse Core Ops, SparseCore 0:
  89.2 75.0 reduce-scatter.4
  166.6 77.2 reduce-scatter.2
  246.8 83.9 all-gather.1
Sparse Core Ops, SparseCore 1:
  252.4 192.9 all-reduce.5
  449.4 102.7 all-reduce.7
